TPU v7x, 32 devices: a whole 2x2x4 slice. The times are simulated.
32 devices in a mesh: rep: 2 (over x), shard: 16 (over z, y, core).
Axes of the slice: x: 2, y: 2, z: 4, core: 2. Of those that a mesh axis runs over, the one named last changes fastest.
Arguments:
- tokens: bfloat16 [32, 192, 2048], P(('rep', 'shard')), may hold values from -7 to 7
- segment_ids: int32 [32, 192], P(('rep', 'shard')), may hold values from 0 to 3, never falling along the last dimension, each value on 1 to 96 neighbouring positions
- norm_gain: bfloat16 [2048], P('shard'), may hold values from 0.25 to 1.75
- input_weight: bfloat16 [2048, 2048], P('shard'), may hold values from -0.125 to 0.125
- forget_weight: bfloat16 [2048, 2048], P('shard'), may hold values from -0.5 to 0.5
- gate_weight: bfloat16 [2048, 2048], P('shard'), may hold values from -0.125 to 0.125
- mixer_gain: bfloat16 [2048], P('shard'), may hold values from 0.25 to 1.75
- out_weight: bfloat16 [2048, 2048], P('shard'), may hold values from -0.1875 to 0.1875
- ffn_gain: bfloat16 [2048], P('shard'), may hold values from 0.25 to 1.75
- ffn_gate_weight: bfloat16 [2048, 5632], P('shard'), may hold values from -0.125 to 0.125
- ffn_up_weight: bfloat16 [2048, 5632], P('shard'), may hold values from -0.125 to 0.125
- ffn_down_weight: bfloat16 [5632, 2048], P('shard'), may hold values from -0.15625 to 0.15625
- cotangent: bfloat16 [32, 192, 2048], P(('rep', 'shard')), may hold values from -6 to 6
Outputs:
- block_output: bfloat16 [32, 192, 2048], P(('rep', 'shard'))
- input_grad: bfloat16 [32, 192, 2048], P(('rep', 'shard'))
- norm_gain_grad: float32 [2048], P('shard')
- input_weight_grad: float32 [2048, 2048], P('shard')
- forget_weight_grad: float32 [2048, 2048], P('shard')
- gate_weight_grad: float32 [2048, 2048], P('shard')
- mixer_gain_grad: float32 [2048], P('shard')
- out_weight_grad: float32 [2048, 2048], P('shard')
- ffn_gain_grad: float32 [2048], P('shard')
- ffn_gate_grad: float32 [2048, 5632], P('shard')
- ffn_up_grad: float32 [2048, 5632], P('shard')
- ffn_down_grad: float32 [5632, 2048], P('shard')
Inputs may be any that keep to these rules, and one draw needn't show every extreme that they name: `segment_ids`: document numbers never fall along a sequence; each document has 1 to 96 tokens, and one has exactly 96.
All inputs are finite; a program needn't handle non-finite values.
Results may differ from a plain program's by a relative error of at most 0.019.
Values may be sent and summed in bfloat16 or wider, within the bound.
No kernel may reach another device: no remote copies, remote signals or barrier semaphores. Data moves between devices by JAX's collectives and lax.ppermute only.
A program may use at most 640 MiB of HBM per device.

v0:
```python
import jax
import jax.numpy as jnp
from jax import lax
from jax.sharding import PartitionSpec as P

EPSILON = 1e-06


def normalize(values):
    scale = lax.rsqrt(jnp.mean(values * values, axis=-1, keepdims=True) + EPSILON)
    return (values * scale, scale)


def norm_back(grad_scaled, scaled, scale):
    inner = jnp.mean(grad_scaled * scaled, axis=-1, keepdims=True)
    return scale * (grad_scaled - scaled * inner)


def swish_pair(values):
    sigma = jax.nn.sigmoid(values)
    return (values * sigma, sigma * (1.0 + values * (1.0 - sigma)))


def combine_steps(earlier, later):
    return (earlier[0] * later[0], later[0] * earlier[1] + later[1])


def linear_scan(decay, update):
    return lax.associative_scan(combine_steps, (decay, update), axis=0)[1]


def contract_rows(left, piece):
    return lax.dot_general(
        left, piece, (((1,), (1,)), ((), ())), preferred_element_type=jnp.float32
    )


def gain_folder(scaled, carry, pieces):
    sums, fulls, gain_full = carry
    gain_piece = pieces[-1]
    matrices = pieces[:-1]
    columns = scaled * gain_piece.astype(jnp.float32)
    lowered = columns.astype(jnp.bfloat16)
    sums = tuple(
        (jnp.dot(lowered, piece, preferred_element_type=jnp.float32) for piece in matrices)
    )
    gain_full = gain_piece
    return (sums, fulls, gain_full)


def plain_folder(lowered_rows, carry, piece):
    total, full = carry
    total = jnp.dot(lowered_rows, piece, preferred_element_type=jnp.float32)
    return (total, full)


def start_carry(length, width, columns, number):
    sums = tuple((jnp.zeros((length, columns), jnp.float32) for index in range(number)))
    fulls = ()
    return (sums, fulls, jnp.zeros((width,), jnp.bfloat16))


def single_columns(left, piece):
    return contract_rows(left, piece)


def multi_columns(lefts, pieces):
    total = contract_rows(lefts[0], pieces[0])
    for left, piece in zip(lefts[1:], pieces[1:]):
        total = total + contract_rows(left, piece)
    return total


def row_grad(left, right):
    return lax.dot_general(
        left, right, (((0,), (0,)), ((), ())), preferred_element_type=jnp.float32
    )


def row_block(pairs, gains):
    pieces = [row_grad(left, right) for left, right in pairs]
    pieces = pieces + [vector[:, None] for vector in gains]
    return jnp.concatenate(pieces, axis=1)


def shards(
    tokens,
    segment_ids,
    norm_gain,
    input_weight,
    forget_weight,
    gate_weight,
    mixer_gain,
    out_weight,
    ffn_gain,
    ffn_gate_weight,
    ffn_up_weight,
    ffn_down_weight,
    cotangent,
):
    inputs = tokens[0].astype(jnp.float32)
    length, width = inputs.shape
    hidden_width = ffn_up_weight.shape[1]
    segments = segment_ids[0]
    same = jnp.concatenate(
        [jnp.zeros((1,), jnp.float32), (segments[1:] == segments[:-1]).astype(jnp.float32)]
    )
    scaled_in, scale_in = normalize(inputs)
    mixer_sums, mixer_full, gain_one = gain_folder(
        scaled_in,
        start_carry(length, width, width, 3),
        (
            lax.all_gather(input_weight, "shard", axis=0, tiled=True),
            lax.all_gather(forget_weight, "shard", axis=0, tiled=True),
            lax.all_gather(gate_weight, "shard", axis=0, tiled=True),
            lax.all_gather(norm_gain, "shard", axis=0, tiled=True),
        ),
    )
    input_pre, forget_pre, gate_pre = mixer_sums
    forget = jax.nn.sigmoid(forget_pre)
    input_act, input_slope = swish_pair(input_pre)
    update = input_act * (1.0 - forget)
    decay = forget * same[:, None]
    state = linear_scan(decay, update)
    state_scaled, state_scale = normalize(state)
    gate_act, gate_slope = swish_pair(gate_pre)
    mixed_pre = state_scaled * gate_act
    out_sums, out_full, gain_two = gain_folder(
        mixed_pre,
        start_carry(length, width, width, 1),
        (
            lax.all_gather(out_weight, "shard", axis=0, tiled=True),
            lax.all_gather(mixer_gain, "shard", axis=0, tiled=True),
        ),
    )
    resid = inputs + out_sums[0]
    scaled_mid, scale_mid = normalize(resid)
    ffn_sums, ffn_full, gain_three = gain_folder(
        scaled_mid,
        start_carry(length, width, hidden_width, 2),
        (
            lax.all_gather(ffn_gate_weight, "shard", axis=0, tiled=True),
            lax.all_gather(ffn_up_weight, "shard", axis=0, tiled=True),
            lax.all_gather(ffn_gain, "shard", axis=0, tiled=True),
        ),
    )
    ffn_gate, ffn_up = ffn_sums
    ffn_act, ffn_slope = swish_pair(ffn_gate)
    hidden = (ffn_act * ffn_up).astype(jnp.bfloat16)
    down_start = (jnp.zeros((length, width), jnp.float32), jnp.zeros((1, 1), jnp.bfloat16))
    ffn_out, down_full = plain_folder(
        hidden, down_start, lax.all_gather(ffn_down_weight, "shard", axis=0, tiled=True)
    )
    block_output = (resid + ffn_out).astype(jnp.bfloat16)
    grad_out = cotangent[0]
    grad_hidden = single_columns(
        grad_out, lax.all_gather(ffn_down_weight, "shard", axis=0, tiled=True)
    )
    grad_fgate = (grad_hidden * ffn_up * ffn_slope).astype(jnp.bfloat16)
    grad_fup = (grad_hidden * ffn_act).astype(jnp.bfloat16)
    grad_ffn_in = multi_columns(
        (grad_fgate, grad_fup),
        lax.all_gather((ffn_gate_weight, ffn_up_weight), "shard", axis=0, tiled=True),
    )
    gain_three_f = gain_three.astype(jnp.float32)
    mid_low = (scaled_mid * gain_three_f).astype(jnp.bfloat16)
    gain_three_grad = jnp.sum(grad_ffn_in * scaled_mid, axis=0)
    grad_resid = grad_out.astype(jnp.float32) + norm_back(
        grad_ffn_in * gain_three_f, scaled_mid, scale_mid
    )
    grad_branch = grad_resid.astype(jnp.bfloat16)
    grad_mixed = single_columns(
        grad_branch, lax.all_gather(out_weight, "shard", axis=0, tiled=True)
    )
    gain_two_f = gain_two.astype(jnp.float32)
    mixed_low = (mixed_pre * gain_two_f).astype(jnp.bfloat16)
    gain_two_grad = jnp.sum(grad_mixed * mixed_pre, axis=0)
    weighted = grad_mixed * gain_two_f
    grad_gate_pre = (weighted * state_scaled * gate_slope).astype(jnp.bfloat16)
    grad_state = norm_back(weighted * gate_act, state_scaled, state_scale)
    next_decay = jnp.concatenate([decay[1:], jnp.zeros((1, width), jnp.float32)])
    carried = jnp.flip(linear_scan(jnp.flip(next_decay, 0), jnp.flip(grad_state, 0)), 0)
    previous = jnp.concatenate([jnp.zeros((1, width), jnp.float32), state[:-1]])
    grad_forget = carried * previous * same[:, None] - carried * input_act
    grad_input_pre = (carried * (1.0 - forget) * input_slope).astype(jnp.bfloat16)
    grad_forget_pre = (grad_forget * forget * (1.0 - forget)).astype(jnp.bfloat16)
    triple = (grad_input_pre, grad_forget_pre, grad_gate_pre)
    grad_normed = multi_columns(
        triple,
        lax.all_gather((input_weight, forget_weight, gate_weight), "shard", axis=0, tiled=True),
    )
    gain_one_f = gain_one.astype(jnp.float32)
    in_low = (scaled_in * gain_one_f).astype(jnp.bfloat16)
    gain_one_grad = jnp.sum(grad_normed * scaled_in, axis=0)
    input_grad = (grad_resid + norm_back(grad_normed * gain_one_f, scaled_in, scale_in)).astype(
        jnp.bfloat16
    )
    triple_joined = jnp.concatenate(triple, axis=1)
    pair_joined = jnp.concatenate([grad_fgate, grad_fup], axis=1)
    pairs = ((in_low, triple_joined), (mixed_low, grad_branch), (mid_low, pair_joined))
    gains = (gain_one_grad, gain_two_grad, gain_three_grad)
    rows_term = lax.psum_scatter(
        row_block(pairs, gains).astype(jnp.bfloat16), "shard", scatter_dimension=0, tiled=True
    )
    down_term = lax.psum_scatter(
        row_grad(hidden, grad_out).astype(jnp.bfloat16), "shard", scatter_dimension=0, tiled=True
    )
    rows_total, down_total = (
        lax.psum(rows_term, "rep").astype(jnp.float32),
        lax.psum(down_term, "rep").astype(jnp.float32),
    )
    tail = 4 * width + 2 * hidden_width
    return (
        block_output[None],
        input_grad[None],
        rows_total[:, tail],
        rows_total[:, :width],
        rows_total[:, width : 2 * width],
        rows_total[:, 2 * width : 3 * width],
        rows_total[:, tail + 1],
        rows_total[:, 3 * width : 4 * width],
        rows_total[:, tail + 2],
        rows_total[:, 4 * width : 4 * width + hidden_width],
        rows_total[:, 4 * width + hidden_width : tail],
        down_total,
    )


def solution(mesh):
    placed = (
        P(("rep", "shard"), None, None),
        P(("rep", "shard"), None),
        P("shard"),
        P("shard", None),
        P("shard", None),
        P("shard", None),
        P("shard"),
        P("shard", None),
        P("shard"),
        P("shard", None),
        P("shard", None),
        P("shard", None),
        P(("rep", "shard"), None, None),
    )
    return jax.shard_map(
        shards,
        mesh=mesh,
        in_specs=placed,
        out_specs=(
            P(("rep", "shard"), None, None),
            P(("rep", "shard"), None, None),
            P("shard"),
            P("shard", None),
            P("shard", None),
            P("shard", None),
            P("shard"),
            P("shard", None),
            P("shard"),
            P("shard", None),
            P("shard", None),
            P("shard", None),
        ),
        check_vma=False,
    )
```

profile of v0, /device:TPU:0, one launch (start us, length us, event | category | flops | bytes accessed | tf_op | source)
XLA Modules:
  0.0 2012.6 jit_solution(17651145178794768228)
XLA Ops:
  12.0 23.2 %all-gather = bf16[16,1,128]{2,1,0:T(2,128)(2,1)S(1)} all-gather(bf16[1,1,128]{2,1,0:T(2,128)(2,1)S(1)} %bitcast.75), channel_id=1, replica_groups=mesh['rep'=2,'shard'=16] {'shard'}, dimensions={0}, use_global_device_ids=true | all-gather | bytes 4352 | tf_op jit(solution)/shard_map/all_gather | solution.py:116
  35.2 17.5 all-gather.1
  52.7 18.9 all-gather.2
  72.6 15.3 all-gather.11.cloned.1.call-done
  94.3 69.0 %all-gather.13.cloned.1.call-done = bf16[2048,2048]{1,0:T(8,128)(2,1)} async-done(((bf16[128,2048]{1,0:T(8,128)(2,1)}), bf16[2048,2048]{1,0:T(8,128)(2,1)}) %all-gather.13.cloned.1.call-update) | async-done | bytes 8388624 | tf_op jit(solution)/shard_map/all_gather | solution.py:114
  163.3 7.8 broadcast_multiply_fusion
  200.5 38.1 %all-gather.15.cloned.1.call-done = bf16[2048,2048]{1,0:T(8,128)(2,1)} async-done(((bf16[128,2048]{1,0:T(8,128)(2,1)}), bf16[2048,2048]{1,0:T(8,128)(2,1)}) %all-gather.15.cloned.1.call-update) | async-done | bytes 8388624 | tf_op jit(solution)/shard_map/all_gather | solution.py:115
  238.6 7.6 multiply_multiply_fusion.1
  246.2 67.6 %all-gather.17.cloned.1.call-done = bf16[2048,2048]{1,0:T(8,128)(2,1)} async-done(((bf16[128,2048]{1,0:T(8,128)(2,1)}), bf16[2048,2048]{1,0:T(8,128)(2,1)}) %all-gather.17.cloned.1.call-update) | async-done | bytes 8388624 | tf_op jit(solution)/shard_map/all_gather | solution.py:132
  322.0 110.3 %all-gather.21.cloned.1.call-done = bf16[2048,5632]{1,0:T(8,128)(2,1)} async-done(((bf16[128,5632]{1,0:T(8,128)(2,1)}), bf16[2048,5632]{1,0:T(8,128)(2,1)}) %all-gather.21.cloned.1.call-update) | async-done | bytes 23068688 | tf_op jit(solution)/shard_map/all_gather | solution.py:143
  432.3 14.5 fusion.74
  446.8 105.7 %all-gather.19.cloned.1.call-done = bf16[2048,5632]{1,0:T(8,128)(2,1)} async-done(((bf16[128,5632]{1,0:T(8,128)(2,1)}), bf16[2048,5632]{1,0:T(8,128)(2,1)}) %all-gather.19.cloned.1.call-update) | async-done | bytes 23068688 | tf_op jit(solution)/shard_map/all_gather | solution.py:142
  552.4 14.7 fusion.73
  567.1 105.7 %all-gather.23.cloned.1.call-done = bf16[5632,2048]{1,0:T(8,128)(2,1)} async-done(((bf16[352,2048]{1,0:T(8,128)(2,1)}), bf16[5632,2048]{1,0:T(8,128)(2,1)}) %all-gather.23.cloned.1.call-update) | async-done | bytes 23068688 | tf_op jit(solution)/shard_map/all_gather | solution.py:152
  672.8 16.0 multiply_convert_fusion
  690.1 10.9 convolution_convert_fusion.1
  717.3 8.6 slice.457
  725.9 8.7 slice.448
  734.6 8.6 slice.450
  745.4 12.1 fusion.75
  757.6 14.4 multiply_reduce_fusion
  775.2 8.6 multiply_reduce_fusion.1
  791.4 8.6 slice.452
  846.6 16.0 rev.6
  866.8 6.8 fusion.76
  887.9 12.3 copy.30
  900.2 13.6 convolution_convert_fusion.2
  913.7 20.9 %convolution_convert_fusion = bf16[2048,11264]{1,0:T(8,128)(2,1)} fusion(bf16[192,2048]{1,0:T(8,128)(2,1)} %multiply_convert_fusion.6, bf16[192,5632]{1,0:T(8,128)(2,1)} %get-tuple-element.29, bf16[192,5632]{1,0:T(8,128)(2,1)} %get-tuple-element.30), kind=kOutput, calls=%fused_computation | convolution fusion | flops 8890089472 | bytes 51249152 | tf_op jit(solution)/shard_map/dot_general | solution.py:75
  934.6 158.1 %concatenate.84 = bf16[2048,19459]{1,0:T(8,128)(2,1)} concatenate(bf16[2048,6144]{1,0:T(8,128)(2,1)} %convolution_convert_fusion.2, bf16[2048,2048]{1,0:T(8,128)(2,1)} %copy.30, bf16[2048,11264]{1,0:T(8,128)(2,1)} %convolution_convert_fusion, bf16[2048,1]{1,0:T(8,128)(2,1)} %broadcast_in_dim.18, bf16[2048,1]{1,0:T(8,128)(2,1)S(1)} %copy-done.24, bf16[2048,1]{1,0:T(8,128)(2,1)S(1)} %copy-done.25), dimensions={1} | concatenate | bytes 159408128 | tf_op jit(solution)/shard_map/concatenate | solution.py:83
  1092.8 743.0 %reduce-scatter.3.cloned.1.call-done = bf16[128,19459]{1,0:T(8,128)(2,1)} async-done(((bf16[2048,19459]{1,0:T(8,128)(2,1)}), bf16[128,19459]{1,0:T(8,128)(2,1)}) %reduce-scatter.3.cloned.1.call-update) | async-done | bytes 4981520 | tf_op jit(solution)/shard_map/reduce_scatter | solution.py:202
  1838.7 12.3 fusion.8
  1851.0 143.4 %all-reduce.33.cloned.1.call-done = (bf16[128,19459]{1,0:T(8,128)(2,1)}, bf16[352,2048]{1,0:T(8,128)(2,1)}) async-done(((bf16[128,19459]{1,0:T(8,128)(2,1)}, bf16[352,2048]{1,0:T(8,128)(2,1)}), (bf16[128,19459]{1,0:T(8,128)(2,1)}, bf16[352,2048]{1,0:T(8,128)(2,1)})) %all-reduce.33.cloned.1.call-update) | async-done | bytes 6423312 | tf_op jit(solution)/shard_map/psum | solution.py:209
  (326 shorter events, 158.2 us)
Async XLA Ops:
  7.2 80.7 %all-gather.11.cloned.1.call-start = ((), (), s32[]{:S(2)}) async-start(), calls=%async_computation.2 | async-start | bytes 8912896 | tf_op jit(solution)/shard_map/all_gather | solution.py:113
  7.9 155.3 %all-gather.13.cloned.1.call-start = ((), (), s32[]{:S(2)}) async-start(), calls=%async_computation.3 | async-start | bytes 8912896 | tf_op jit(solution)/shard_map/all_gather | solution.py:114
  8.7 229.9 %all-gather.15.cloned.1.call-start = ((), (), s32[]{:S(2)}) async-start(), calls=%async_computation.4 | async-start | bytes 8912896 | tf_op jit(solution)/shard_map/all_gather | solution.py:115
  9.4 304.4 %all-gather.17.cloned.1.call-start = ((), (), s32[]{:S(2)}) async-start(), calls=%async_computation.5 | async-start | bytes 8912896 | tf_op jit(solution)/shard_map/all_gather | solution.py:132
  10.0 422.3 %all-gather.21.cloned.1.call-start = ((), (), s32[]{:S(2)}) async-start(), calls=%async_computation.7 | async-start | bytes 24510464 | tf_op jit(solution)/shard_map/all_gather | solution.py:143
  10.6 24.7 %copy-start.46 = (bf16[128]{0:T(256)(128)(2,1)S(1)}, bf16[128]{0:T(256)(128)(2,1)}, u32[]{:S(2)}) copy-start(bf16[128]{0:T(256)(128)(2,1)} %param.19) | copy-start | bytes 772
  10.6 42.1 %copy-start.47 = (bf16[128]{0:T(256)(128)(2,1)S(1)}, bf16[128]{0:T(256)(128)(2,1)}, u32[]{:S(2)}) copy-start(bf16[128]{0:T(256)(128)(2,1)} %param.21) | copy-start | bytes 772
  10.6 61.6 %copy-start.44 = (s32[1,192]{1,0:T(1,128)S(1)}, s32[1,192]{1,0:T(1,128)}, u32[]{:S(2)}) copy-start(s32[1,192]{1,0:T(1,128)} %param.14) | copy-start | bytes 2308
  10.6 61.8 %copy-start.1 = (bf16[1,192,2048]{2,1,0:T(8,128)(2,1)S(1)}, bf16[1,192,2048]{2,1,0:T(8,128)(2,1)}, u32[]{:S(2)}) copy-start(bf16[1,192,2048]{2,1,0:T(8,128)(2,1)} %param.13) | copy-start | bytes 2359300
  10.6 541.8 %all-gather.19.cloned.1.call-start = ((), (), s32[]{:S(2)}) async-start(), calls=%async_computation.6 | async-start | bytes 24510464 | tf_op jit(solution)/shard_map/all_gather | solution.py:142
  11.2 661.6 %all-gather.23.cloned.1.call-start = ((), (), s32[]{:S(2)}) async-start(), calls=%async_computation.8 | async-start | bytes 24510464 | tf_op jit(solution)/shard_map/all_gather | solution.py:152
  11.9 1080.8 %reduce-scatter.5.cloned.1.call-start = ((), (), s32[]{:S(2)}) async-start(), calls=%async_computation.10 | async-start | bytes 24510464 | tf_op jit(solution)/shard_map/reduce_scatter | solution.py:205
  72.4 90.9 %copy-start.42 = (f32[192]{0:T(256)}, f32[192]{0:T(256)S(1)}, u32[]{:S(2)}) copy-start(f32[192]{0:T(256)S(1)} %add_convert_fusion) | copy-start | bytes 2308
  72.6 90.6 %copy-start.32 = (f32[192]{0:T(256)}, f32[192]{0:T(256)S(1)}, u32[]{:S(2)}) copy-start(f32[192]{0:T(256)S(1)} %add_rsqrt_fusion.2) | copy-start | bytes 2308
  175.9 6.0 copy-start.10
  199.1 39.5 %copy-start.33 = (f32[192]{0:T(256)S(1)}, f32[192]{0:T(256)}, u32[]{:S(2)}) copy-start(f32[192]{0:T(256)} %copy-done.32) | copy-start | bytes 2308
  313.8 7.1 copy-start.31
  672.8 17.3 copy-start.20
  701.1 1134.7 %reduce-scatter.3.cloned.1.call-start = ((), (), s32[]{:S(2)}) async-start(), calls=%async_computation.9 | async-start | bytes 85229568 | tf_op jit(solution)/shard_map/reduce_scatter | solution.py:202
  745.4 12.2 copy-start.6
  791.4 8.7 copy-start.15
  819.0 5.8 copy-start.14
  822.9 7.7 copy-start.41
  846.6 16.0 copy-start.43
  862.6 11.0 slice-start
  866.8 6.9 copy-start.12
  866.8 6.9 slice-start.1
  866.8 9.8 slice-start.2
  876.6 5.4 copy-start.22
  913.7 20.9 %copy-start.24 = (bf16[2048,1]{1,0:T(8,128)(2,1)S(1)}, bf16[2048,1]{1,0:T(8,128)(2,1)}, u32[]{:S(2)}) copy-start(bf16[2048,1]{1,0:T(8,128)(2,1)} %broadcast_in_dim.19) | copy-start | bytes 12292
  913.7 20.9 %copy-start.25 = (bf16[2048,1]{1,0:T(8,128)(2,1)S(1)}, bf16[2048,1]{1,0:T(8,128)(2,1)}, u32[]{:S(2)}) copy-start(bf16[2048,1]{1,0:T(8,128)(2,1)} %broadcast_in_dim.20) | copy-start | bytes 12292
  1092.7 901.7 %all-reduce.33.cloned.1.call-start = ((), (), s32[]{:S(2)}) async-start(), calls=%async_computation.11 | async-start | bytes 12910592 | tf_op jit(solution)/shard_map/psum | solution.py:209
  (30 other events, 60.0 us)
Sparse Core Ops, SparseCore 0:
  10.2 77.6 all-gather.10
  90.1 73.1 all-gather.12
  165.4 73.1 all-gather.14
  240.6 73.1 all-gather.16
  315.3 116.9 all-gather.20
  433.7 118.6 all-gather.18
  554.0 118.6 all-gather.22
  701.2 226.8 reduce-scatter.4
  1092.8 742.9 reduce-scatter.2
  1838.2 156.2 all-reduce.32
where the time goes:
time: 2030 us; the launch traced here: 2010 us
  waiting for transfers between devices  1400 us (69%)
  local copies, waits for them, and re-layouts  319 us (16%)
  matrix products  185 us (9%)
  blocking collectives  59.6 us (3%)
  other arithmetic  30.4 us (1%)
    reduce_scatter x1, waiting for transfers between devices, shards(): lax.psum_scatter(row_block(pairs, gains).astype(jnp.bfloat16), 'shard', s...  743 us
    concatenate x1, local copies, waits for them, and re-layouts, row_block(): return jnp.concatenate(pieces, axis=1)  158 us
    psum x1, waiting for transfers between devices, shards(): lax.psum(rows_term, 'rep').astype(jnp.float32)  143 us
    all_gather x1, waiting for transfers between devices, shards(): lax.all_gather(ffn_up_weight, 'shard', axis=0, tiled=True)  110 us
    all_gather x1, waiting for transfers between devices, shards(): lax.all_gather(ffn_gate_weight, 'shard', axis=0, tiled=True)  106 us
    all_gather x1, waiting for transfers between devices, shards(): lax.all_gather(ffn_down_weight, 'shard', axis=0, tiled=True)  106 us
    slice x90, local copies, waits for them, and re-layouts, linear_scan(): return lax.associative_scan(combine_steps, (decay, update), axis=0)[1]  96.4 us
    all_gather x1, waiting for transfers between devices, shards(): lax.all_gather(forget_weight, 'shard', axis=0, tiled=True)  69 us
  transfers between devices with their start and end apart: 10, of which 9 were waited for; matrix products, arithmetic and copies ran while one was open for 24% of the time, Pallas kernels for 0%

commit v1 on v0

--- a/solution.py
+++ b/solution.py
@@ -4,6 +4,27 @@
 from jax.sharding import PartitionSpec as P
 
 EPSILON = 1e-06
+
+
+def laid_out(parts, dim):
+    lengths = list(parts.shape[1:])
+    lengths[dim] *= parts.shape[0]
+    return jnp.moveaxis(parts, 0, dim).reshape(lengths)
+
+
+def grow_blocks(shard, axis):
+    devices, index = (lax.axis_size(axis), lax.axis_index(axis))
+    blocks, bit = (shard[None], 1)
+    while bit < devices:
+        other = lax.ppermute(blocks, axis, [(i, i ^ bit) for i in range(devices)])
+        low = index & bit == 0
+        blocks = jnp.concatenate([jnp.where(low, blocks, other), jnp.where(low, other, blocks)])
+        bit *= 2
+    return blocks
+
+
+def doubled_up(array, axis, dim):
+    return laid_out(grow_blocks(array, axis), dim)
 
 
 def normalize(values):
@@ -148,9 +169,7 @@
     ffn_act, ffn_slope = swish_pair(ffn_gate)
     hidden = (ffn_act * ffn_up).astype(jnp.bfloat16)
     down_start = (jnp.zeros((length, width), jnp.float32), jnp.zeros((1, 1), jnp.bfloat16))
-    ffn_out, down_full = plain_folder(
-        hidden, down_start, lax.all_gather(ffn_down_weight, "shard", axis=0, tiled=True)
-    )
+    ffn_out, down_full = plain_folder(hidden, down_start, doubled_up(ffn_down_weight, "shard", 0))
     block_output = (resid + ffn_out).astype(jnp.bfloat16)
     grad_out = cotangent[0]
     grad_hidden = single_columns(

time: 2030 us -> 2470 us (1.22)
  waiting for transfers between devices: 1400 us -> 1780 us
  other arithmetic: 30.4 us -> 86.2 us
    ppermute x0 -> x4, waiting for transfers between devices: none -> 318 us  [grow_blocks(): other = lax.ppermute(blocks, axis, [(i, i ^ bit) for i in range(devices)])]
    reduce_scatter x1, waiting for transfers between devices: 743 us -> 840 us  [shards(): lax.psum_scatter(row_block(pairs, gains).astype(jnp.bfloat16), 'shard', s...]
    psum x1, waiting for transfers between devices: 143 us -> 107 us  [shards(): lax.psum(rows_term, 'rep').astype(jnp.float32)]
    concatenate x0 -> x4, other arithmetic: none -> 31.5 us  [grow_blocks(): jnp.concatenate([jnp.where(low, blocks, other), jnp.where(low, other, blo...]
    select_n x0 -> x4, other arithmetic: none -> 25.8 us  [grow_blocks(): jnp.where(low, blocks, other)]
  transfers between devices with their start and end apart: 10 -> 14, of which waited for: 9 -> 12; matrix products, arithmetic and copies ran while one was open for 24% -> 22% of each run, Pallas kernels for 0% -> 0%
where the time goes in v1:
time: 2470 us; the launch traced here: 2460 us
  waiting for transfers between devices  1780 us (72%)
  local copies, waits for them, and re-layouts  325 us (13%)
  matrix products  184 us (7%)
  other arithmetic  86.2 us (3%)
  blocking collectives  59.6 us (2%)
    reduce_scatter x1, waiting for transfers between devices, shards(): lax.psum_scatter(row_block(pairs, gains).astype(jnp.bfloat16), 'shard', s...  840 us
    ppermute x4, waiting for transfers between devices, grow_blocks(): other = lax.ppermute(blocks, axis, [(i, i ^ bit) for i in range(devices)])  318 us
    concatenate x1, local copies, waits for them, and re-layouts, row_block(): return jnp.concatenate(pieces, axis=1)  158 us
    all_gather x1, waiting for transfers between devices, shards(): lax.all_gather(ffn_up_weight, 'shard', axis=0, tiled=True)  110 us
    psum x1, waiting for transfers between devices, shards(): lax.psum(rows_term, 'rep').astype(jnp.float32)  107 us
    all_gather x1, waiting for transfers between devices, shards(): lax.all_gather(ffn_gate_weight, 'shard', axis=0, tiled=True)  106 us
    all_gather x1, waiting for transfers between devices, shards(): lax.all_gather(ffn_down_weight, 'shard', axis=0, tiled=True)  106 us
    slice x90, local copies, waits for them, and re-layouts, linear_scan(): return lax.associative_scan(combine_steps, (decay, update), axis=0)[1]  96.5 us
  transfers between devices with their start and end apart: 14, of which 12 were waited for; matrix products, arithmetic and copies ran while one was open for 22% of the time, Pallas kernels for 0%

profile of v1, /device:TPU:0, one launch (start us, length us, event | category | flops | bytes accessed | tf_op | source)
XLA Modules:
  0.0 2458.2 jit_solution(6857953637173491173)
XLA Ops:
  12.0 23.2 all-gather
  35.2 17.5 all-gather.1
  52.7 18.9 all-gather.2
  72.6 15.3 all-gather.11.cloned.1.call-done
  94.3 69.0 %all-gather.13.cloned.1.call-done = bf16[2048,2048]{1,0:T(8,128)(2,1)} async-done(((bf16[128,2048]{1,0:T(8,128)(2,1)}), bf16[2048,2048]{1,0:T(8,128)(2,1)}) %all-gather.13.cloned.1.call-update) | async-done | bytes 8388624 | tf_op jit(solution)/shard_map/all_gather | solution.py:135
  200.5 38.1 %all-gather.15.cloned.1.call-done = bf16[2048,2048]{1,0:T(8,128)(2,1)} async-done(((bf16[128,2048]{1,0:T(8,128)(2,1)}), bf16[2048,2048]{1,0:T(8,128)(2,1)}) %all-gather.15.cloned.1.call-update) | async-done | bytes 8388624 | tf_op jit(solution)/shard_map/all_gather | solution.py:136
  246.4 67.5 %all-gather.17.cloned.1.call-done = bf16[2048,2048]{1,0:T(8,128)(2,1)} async-done(((bf16[128,2048]{1,0:T(8,128)(2,1)}), bf16[2048,2048]{1,0:T(8,128)(2,1)}) %all-gather.17.cloned.1.call-update) | async-done | bytes 8388624 | tf_op jit(solution)/shard_map/all_gather | solution.py:153
  322.1 110.2 %all-gather.21.cloned.1.call-done = bf16[2048,5632]{1,0:T(8,128)(2,1)} async-done(((bf16[128,5632]{1,0:T(8,128)(2,1)}), bf16[2048,5632]{1,0:T(8,128)(2,1)}) %all-gather.21.cloned.1.call-update) | async-done | bytes 23068688 | tf_op jit(solution)/shard_map/all_gather | solution.py:164
  432.3 14.4 fusion.74
  446.7 105.7 %all-gather.19.cloned.1.call-done = bf16[2048,5632]{1,0:T(8,128)(2,1)} async-done(((bf16[128,5632]{1,0:T(8,128)(2,1)}), bf16[2048,5632]{1,0:T(8,128)(2,1)}) %all-gather.19.cloned.1.call-update) | async-done | bytes 23068688 | tf_op jit(solution)/shard_map/all_gather | solution.py:163
  552.5 14.7 fusion.73
  567.1 105.7 %all-gather.23.cloned.1.call-done = bf16[5632,2048]{1,0:T(8,128)(2,1)} async-done(((bf16[352,2048]{1,0:T(8,128)(2,1)}), bf16[5632,2048]{1,0:T(8,128)(2,1)}) %all-gather.23.cloned.1.call-update) | async-done | bytes 23068688 | tf_op jit(solution)/shard_map/all_gather | solution.py:176
  672.8 16.0 multiply_convert_fusion
  690.2 10.8 convolution_convert_fusion.1
  717.2 8.6 slice.457
  725.9 8.7 slice.448
  734.5 8.6 slice.450
  745.3 12.1 fusion.75
  757.5 14.4 multiply_reduce_fusion
  791.5 8.7 slice.452
  846.9 16.1 rev.6
  888.2 12.4 copy.30
  900.7 12.3 convolution_convert_fusion.2
  913.0 20.9 convolution_convert_fusion
  933.9 157.9 %concatenate.100 = bf16[2048,19459]{1,0:T(8,128)(2,1)} concatenate(bf16[2048,6144]{1,0:T(8,128)(2,1)} %convolution_convert_fusion.2, bf16[2048,2048]{1,0:T(8,128)(2,1)} %copy.30, bf16[2048,11264]{1,0:T(8,128)(2,1)} %convolution_convert_fusion, bf16[2048,1]{1,0:T(8,128)(2,1)S(1)} %copy-done.38, bf16[2048,1]{1,0:T(8,128)(2,1)S(1)} %copy-done.36, bf16[2048,1]{1,0:T(8,128)(2,1)S(1)} %copy-done.37), dimensions={1} | concatenate | bytes 159408128 | tf_op jit(solution)/shard_map/concatenate | solution.py:104
  1099.5 63.4 %collective-permute-done.1 = bf16[2,352,2048]{2,1,0:T(8,128)(2,1)} collective-permute-done((bf16[2,352,2048]{2,1,0:T(8,128)(2,1)S(1)}, bf16[2,352,2048]{2,1,0:T(8,128)(2,1)}, u32[]{:S(2)}, u32[]{:S(2)}) %collective-permute-start.1) | collective-permute-done | bytes 2883616 | tf_op jit(solution)/shard_map/ppermute | solution.py:19
  1173.7 251.8 %collective-permute-done.2 = bf16[4,352,2048]{2,1,0:T(8,128)(2,1)} collective-permute-done((bf16[4,352,2048]{2,1,0:T(8,128)(2,1)}, bf16[4,352,2048]{2,1,0:T(8,128)(2,1)}, u32[]{:S(2)}, u32[]{:S(2)}) %collective-permute-start.2) | collective-permute-done | bytes 5767200 | tf_op jit(solution)/shard_map/ppermute | solution.py:19
  1441.1 839.7 %reduce-scatter.3.cloned.1.call-done = bf16[128,19459]{1,0:T(8,128)(2,1)} async-done(((bf16[2048,19459]{1,0:T(8,128)(2,1)}), bf16[128,19459]{1,0:T(8,128)(2,1)}) %reduce-scatter.3.cloned.1.call-update) | async-done | bytes 4981520 | tf_op jit(solution)/shard_map/reduce_scatter | solution.py:221
  2280.8 17.0 broadcast_select_fusion.1
  2297.8 20.8 pad_maximum_fusion
  2321.0 11.6 fusion.8
  2332.6 107.4 %all-reduce.33.cloned.1.call-done = (bf16[128,19459]{1,0:T(8,128)(2,1)}, bf16[352,2048]{1,0:T(8,128)(2,1)}) async-done(((bf16[128,19459]{1,0:T(8,128)(2,1)}, bf16[352,2048]{1,0:T(8,128)(2,1)}), (bf16[128,19459]{1,0:T(8,128)(2,1)}, bf16[352,2048]{1,0:T(8,128)(2,1)})) %all-reduce.33.cloned.1.call-update) | async-done | bytes 6423312 | tf_op jit(solution)/shard_map/psum | solution.py:228
  (368 shorter events, 223.1 us)
Async XLA Ops:
  7.2 80.7 %all-gather.11.cloned.1.call-start = ((), (), s32[]{:S(2)}) async-start(), calls=%async_computation.2 | async-start | bytes 8912896 | tf_op jit(solution)/shard_map/all_gather | solution.py:134
  7.9 155.3 %all-gather.13.cloned.1.call-start = ((), (), s32[]{:S(2)}) async-start(), calls=%async_computation.3 | async-start | bytes 8912896 | tf_op jit(solution)/shard_map/all_gather | solution.py:135
  8.7 229.9 %all-gather.15.cloned.1.call-start = ((), (), s32[]{:S(2)}) async-start(), calls=%async_computation.4 | async-start | bytes 8912896 | tf_op jit(solution)/shard_map/all_gather | solution.py:136
  9.4 304.4 %all-gather.17.cloned.1.call-start = ((), (), s32[]{:S(2)}) async-start(), calls=%async_computation.5 | async-start | bytes 8912896 | tf_op jit(solution)/shard_map/all_gather | solution.py:153
  10.0 422.3 %all-gather.21.cloned.1.call-start = ((), (), s32[]{:S(2)}) async-start(), calls=%async_computation.7 | async-start | bytes 24510464 | tf_op jit(solution)/shard_map/all_gather | solution.py:164
  10.6 24.7 %copy-start.59 = (bf16[128]{0:T(256)(128)(2,1)S(1)}, bf16[128]{0:T(256)(128)(2,1)}, u32[]{:S(2)}) copy-start(bf16[128]{0:T(256)(128)(2,1)} %param.19) | copy-start | bytes 772
  10.6 42.1 %copy-start.60 = (bf16[128]{0:T(256)(128)(2,1)S(1)}, bf16[128]{0:T(256)(128)(2,1)}, u32[]{:S(2)}) copy-start(bf16[128]{0:T(256)(128)(2,1)} %param.21) | copy-start | bytes 772
  10.6 61.6 %copy-start.57 = (s32[1,192]{1,0:T(1,128)S(1)}, s32[1,192]{1,0:T(1,128)}, u32[]{:S(2)}) copy-start(s32[1,192]{1,0:T(1,128)} %param.14) | copy-start | bytes 2308
  10.6 61.8 %copy-start.8 = (bf16[1,192,2048]{2,1,0:T(8,128)(2,1)S(1)}, bf16[1,192,2048]{2,1,0:T(8,128)(2,1)}, u32[]{:S(2)}) copy-start(bf16[1,192,2048]{2,1,0:T(8,128)(2,1)} %param.13) | copy-start | bytes 2359300
  10.6 541.8 %all-gather.19.cloned.1.call-start = ((), (), s32[]{:S(2)}) async-start(), calls=%async_computation.6 | async-start | bytes 24510464 | tf_op jit(solution)/shard_map/all_gather | solution.py:163
  11.2 661.6 %all-gather.23.cloned.1.call-start = ((), (), s32[]{:S(2)}) async-start(), calls=%async_computation.8 | async-start | bytes 24510464 | tf_op jit(solution)/shard_map/all_gather | solution.py:176
  11.9 1429.1 %reduce-scatter.5.cloned.1.call-start = ((), (), s32[]{:S(2)}) async-start(), calls=%async_computation.10 | async-start | bytes 24510464 | tf_op jit(solution)/shard_map/reduce_scatter | solution.py:224
  72.4 90.9 %copy-start.55 = (f32[192]{0:T(256)}, f32[192]{0:T(256)S(1)}, u32[]{:S(2)}) copy-start(f32[192]{0:T(256)S(1)} %add_convert_fusion) | copy-start | bytes 2308
  72.6 90.6 %copy-start.45 = (f32[192]{0:T(256)}, f32[192]{0:T(256)S(1)}, u32[]{:S(2)}) copy-start(f32[192]{0:T(256)S(1)} %add_rsqrt_fusion.2) | copy-start | bytes 2308
  199.2 39.4 %copy-start.46 = (f32[192]{0:T(256)S(1)}, f32[192]{0:T(256)}, u32[]{:S(2)}) copy-start(f32[192]{0:T(256)} %copy-done.45) | copy-start | bytes 2308
  672.8 17.4 copy-start.32
  701.0 1579.8 %reduce-scatter.3.cloned.1.call-start = ((), (), s32[]{:S(2)}) async-start(), calls=%async_computation.9 | async-start | bytes 85229568 | tf_op jit(solution)/shard_map/reduce_scatter | solution.py:221
  774.1 108.3 %copy-start.4 = (f32[192,2048]{1,0:T(8,128)}, f32[192,2048]{1,0:T(8,128)S(1)}, u32[]{:S(2)}) copy-start(f32[192,2048]{1,0:T(8,128)S(1)} %multiply_add_fusion) | copy-start | bytes 4718596
  846.9 16.1 copy-start.56
  888.2 12.5 copy-start.22
  888.2 12.5 copy-start.24
  913.0 20.9 copy-start.36
  913.0 20.9 copy-start.37
  913.0 20.9 copy-start.38
  1091.8 1348.3 %all-reduce.33.cloned.1.call-start = ((), (), s32[]{:S(2)}) async-start(), calls=%async_computation.11 | async-start | bytes 12910592 | tf_op jit(solution)/shard_map/psum | solution.py:228
  1093.1 3.2 collective-permute-start
  1098.1 64.7 %collective-permute-start.1 = (bf16[2,352,2048]{2,1,0:T(8,128)(2,1)S(1)}, bf16[2,352,2048]{2,1,0:T(8,128)(2,1)}, u32[]{:S(2)}, u32[]{:S(2)}) collective-permute-start(bf16[2,352,2048]{2,1,0:T(8,128)(2,1)S(1)} %pad_maximum_fusion.3), channel_id=1, source_target_pairs={{0,2},{1,3},{2,0},{3,1},{4,6},{5,7},{6,4},{7,5},{8,10},{9,11},{10,... | collective-permute-start | bytes 8650760 | tf_op jit(solution)/shard_map/ppermute | solution.py:19
  1172.2 253.3 %collective-permute-start.2 = (bf16[4,352,2048]{2,1,0:T(8,128)(2,1)}, bf16[4,352,2048]{2,1,0:T(8,128)(2,1)}, u32[]{:S(2)}, u32[]{:S(2)}) collective-permute-start(bf16[4,352,2048]{2,1,0:T(8,128)(2,1)} %pad_maximum_fusion.2), channel_id=1, source_target_pairs={{0,4},{1,5},{2,6},{3,7},{4,0},{5,1},{6,2},{7,3},{8,12},{9,13},{10,... | collective-permute-start | bytes 17301512 | tf_op jit(solution)/shard_map/ppermute | solution.py:19
  1437.6 843.2 %collective-permute-start.3 = (bf16[8,352,2048]{2,1,0:T(8,128)(2,1)}, bf16[8,352,2048]{2,1,0:T(8,128)(2,1)}, u32[]{:S(2)}, u32[]{:S(2)}) collective-permute-start(bf16[8,352,2048]{2,1,0:T(8,128)(2,1)} %pad_maximum_fusion.1), channel_id=1, source_target_pairs={{0,8},{1,9},{2,10},{3,11},{4,12},{5,13},{6,14},{7,15},{8,0},{9,1},... | collective-permute-start | bytes 34603016 | tf_op jit(solution)/shard_map/ppermute | solution.py:19
  2297.8 20.8 copy-start.5
  2297.8 20.8 copy-start.10
  2297.8 20.8 copy-start.16
  (47 other events, 169.1 us)
Sparse Core Ops, SparseCore 0:
  10.2 77.6 all-gather.10
  90.1 73.1 all-gather.12
  165.4 73.1 all-gather.14
  240.6 73.1 all-gather.16
  315.3 116.9 all-gather.20
  433.7 118.6 all-gather.18
  554.0 118.6 all-gather.22
  701.1 226.8 reduce-scatter.4
  1091.9 1188.7 reduce-scatter.2
  2283.1 156.8 all-reduce.32
